TPU v7x, 32 devices: a whole 2x2x4 slice. The times are simulated.
32 devices in a mesh: section: 4 (over y, x), fsdp: 8 (over z, core).
Axes of the slice: x: 2, y: 2, z: 4, core: 2. Of those that a mesh axis runs over, the one named last changes fastest.
Arguments:
- enc_states: bfloat16 [8, 4, 1280], P('fsdp'), may hold values from -6 to 6
- clip_frames: int32 [8], replicated, may hold values from 2 to 4, as said below
- clip_offset: int32 [8], replicated, may hold values from 0 to 126, as said below
- ln_gain: float32 [1280], replicated, may hold values from 0.1 to 1.9
- ln_bias: float32 [1280], replicated, may hold values from -0.6 to 0.6
- w_proj: bfloat16 [1280, 8192], P(None, 'fsdp'), may hold values from -0.15625 to 0.15625
- proj_bias: float32 [8192], P('fsdp'), may hold values from -3 to 3
- text_embed: bfloat16 [64, 2, 8192], P(None, None, 'fsdp'), may hold values from -6 to 6
- norm_gain: float32 [4, 8192], P('section'), may hold values from 0.1 to 1.9
- w_gate: bfloat16 [4, 14784, 8192], P('section', 'fsdp'), may hold values from -0.0625 to 0.0625
- w_up: bfloat16 [4, 14784, 8192], P('section', 'fsdp'), may hold values from -0.0625 to 0.0625
- w_down: bfloat16 [4, 14784, 8192], P('section', 'fsdp'), may hold values from -0.046875 to 0.046875
Outputs:
- stream_out: bfloat16 [64, 2, 8192], P('section', None, 'fsdp')
Inputs may be any that keep to these rules, and one draw needn't show every extreme that they name: `clip_frames`: every clip's frame count is even, and some clip has exactly 4 frames. Clip c's live rows occupy stream positions clip_offset[c] to clip_offset[c] + clip_frames[c] / 2 - 1, all inside one microbatch (positions m * 64 to (m + 1) * 64 - 1); no two clips share a position; each microbatch holds 4 clips.
All inputs are finite; a program needn't handle non-finite values.
Results may differ from a plain program's by a relative error of at most 0.015.
Values may be sent and summed in bfloat16 or wider, within the bound.
No kernel may reach another device: no remote copies, remote signals or barrier semaphores. Data moves between devices by JAX's collectives and lax.ppermute only.
A program may use at most 192 MiB of HBM per device.

v0:
```python
import jax
import jax.numpy as jnp
from jax import lax
from jax.sharding import PartitionSpec as P


def from_behind(value, axis, steps):
    count = lax.axis_size(axis)
    initial, last = (max(0, -steps), min(count, count - steps))
    return lax.ppermute(value, axis, [(source, source + steps) for source in range(initial, last)])


def from_root(value, axis, source):
    kept = jnp.where(lax.axis_index(axis) == source, value, 0).astype(value.dtype)
    return lax.psum(kept, axis)


def rms_scaled(stream, gain):
    values = stream.astype(jnp.float32)
    scale = lax.rsqrt(jnp.mean(values * values, axis=-1, keepdims=True) + 1e-06)
    return (values * scale * gain).astype(jnp.bfloat16)


def on_device(
    enc_states,
    clip_frames,
    clip_offset,
    ln_gain,
    ln_bias,
    w_proj,
    proj_bias,
    text_embed,
    norm_gain,
    w_gate,
    w_up,
    w_down,
):
    section_count = lax.axis_size("section")
    section_index = lax.axis_index("section")
    local_clips, frame_len, enc_width = enc_states.shape
    clip_rows = frame_len // 2
    tokens, micro, feat_local = text_embed.shape
    slots = tokens * micro
    pairs = enc_states.astype(jnp.float32).reshape(local_clips, clip_rows, 2, enc_width)
    pooled = 0.5 * (pairs[:, :, 0] + pairs[:, :, 1])
    centre = jnp.mean(pooled, axis=-1, keepdims=True)
    centred = pooled - centre
    spread = jnp.mean(centred * centred, axis=-1, keepdims=True)
    audio_ln = (centred * lax.rsqrt(spread + 1e-05) * ln_gain + ln_bias).astype(jnp.bfloat16)
    audio_ln = audio_ln.reshape(local_clips * clip_rows, enc_width)
    summed = jnp.dot(
        lax.all_gather(audio_ln, "fsdp", axis=0, tiled=True),
        w_proj,
        preferred_element_type=jnp.float32,
    )
    projected = (summed + proj_bias).astype(jnp.bfloat16)
    within = jnp.arange(clip_rows, dtype=jnp.int32)
    live = within[None, :] * 2 < clip_frames[:, None]
    spot = clip_offset[:, None] + within[None, :]
    target = jnp.where(live, spot % tokens * micro + spot // tokens, slots).reshape(-1)
    flags = jnp.zeros((slots,), jnp.int32).at[target].set(1, mode="drop").reshape(tokens, micro)
    placed = jnp.zeros((slots, feat_local), jnp.bfloat16).at[target].set(projected, mode="drop")
    placed = placed.reshape(tokens, micro, feat_local)
    embedded = jnp.where(flags[:, :, None] == 1, placed, text_embed)
    gain = norm_gain[0]
    gate_w = w_gate[0]
    up_w = w_up[0]
    down_w = w_down[0]
    width = gate_w.shape[1]
    dims = (((1,), (1,)), ((), ()))
    group = 1
    waves = micro // group
    turns = waves + section_count - 1
    zero_rows = jnp.zeros((tokens, group, feat_local), jnp.bfloat16)
    incoming = zero_rows
    finished = jnp.zeros((tokens, micro, feat_local), jnp.bfloat16)
    first_section = section_index == 0
    for turn in range(turns):
        if turn < waves:
            fresh = embedded[:, turn * group : (turn + 1) * group]
        else:
            fresh = zero_rows
        current = jnp.where(first_section, fresh, incoming)
        whole = lax.all_gather(current, "fsdp", axis=2, tiled=True)
        layer_normed = rms_scaled(whole, gain).reshape(-1, width)
        gate = lax.dot_general(layer_normed, gate_w, dims, preferred_element_type=jnp.float32)
        up = lax.dot_general(layer_normed, up_w, dims, preferred_element_type=jnp.float32)
        hidden = (jax.nn.silu(gate) * up).astype(jnp.bfloat16)
        partial_sum = jnp.dot(hidden, down_w, preferred_element_type=jnp.float32).reshape(
            tokens, group, width
        )
        branch = lax.psum_scatter(partial_sum, "fsdp", scatter_dimension=2, tiled=True)
        output = (current.astype(jnp.float32) + branch).astype(jnp.bfloat16)
        leaving = turn - (section_count - 1)
        if leaving >= 0:
            finished = finished.at[:, leaving * group : (leaving + 1) * group].set(output)
        if turn + 1 < turns:
            incoming = from_behind(output, "section", 1)
    complete = from_root(finished, "section", section_count - 1)
    rows_each = tokens // section_count
    return lax.dynamic_slice_in_dim(complete, section_index * rows_each, rows_each, 0)


def solution(mesh):
    placed = (
        P("fsdp", None, None),
        P(),
        P(),
        P(),
        P(),
        P(None, "fsdp"),
        P("fsdp"),
        P(None, None, "fsdp"),
        P("section", None),
        P("section", "fsdp", None),
        P("section", "fsdp", None),
        P("section", "fsdp", None),
    )
    return jax.shard_map(
        on_device, mesh=mesh, in_specs=placed, out_specs=P("section", None, "fsdp"), check_vma=False
    )
```

profile of v0, /device:TPU:0, one launch (start us, length us, event | category | flops | bytes accessed | tf_op | source)
XLA Modules:
  0.0 612.4 jit_solution(13028541609225380550)
XLA Ops:
  6.6 0.9 reshape.455
  7.4 0.1 fusion.172
  7.6 0.2 fusion.159
  7.7 0.8 fusion.160
  8.5 15.8 %all-gather = bf16[8,2,1280]{2,1,0:T(2,128)(2,1)S(1)} all-gather(bf16[1,2,1280]{2,1,0:T(2,128)(2,1)S(1)} %fusion.160), channel_id=1, replica_groups=mesh['section'=4,'fsdp'=8] {'fsdp'}, dimensions={0}, use_global_device_ids=true | all-gather | bytes 46080 | tf_op jit(solution)/shard_map/all_gather | solution.py:52
  24.3 0.7 iota_add_fusion
  25.1 0.7 broadcast_compare_fusion
  26.0 1.1 fusion.100
  27.1 0.8 scatter_custom_fusion.1
  27.9 0.1 reshape.443
  28.0 0.6 scatter_custom_fusion
  28.7 0.1 eq.26
  28.9 0.2 copy_select_fusion
  29.1 0.7 slice_select_fusion
  29.8 23.4 %all-gather.7.cloned.1.call-done = bf16[64,1,8192]{2,0,1:T(8,128)(2,1)} async-done(((bf16[64,1,1024]{2,0,1:T(8,128)(2,1)}), bf16[64,1,8192]{2,0,1:T(8,128)(2,1)}) %all-gather.7.cloned.1.call-update) | async-done | bytes 1048592 | tf_op jit(solution)/shard_map/all_gather | solution.py:84
  53.2 1.6 fusion.85
  54.9 14.8 %fusion.28 = f32[64,1848]{1,0:T(8,128)S(1)} fusion(bf16[1,1848,8192]{2,1,0:T(8,128)(2,1)} %param.25, bf16[64,1,8192]{2,0,1:T(8,128)(2,1)S(1)} %copy-done.2, f32[8192]{0:T(1024)S(1)} %bitcast.133, f32[64]{0:T(128)S(1)} %add_rsqrt_fusion.4), kind=kOutput, calls=%fused_computation.30 | convolution fusion | flops 1939865600 | bytes 31832320 | tf_op jit(solution)/shard_map/dot_general | solution.py:86
  69.7 25.7 %fusion.30 = f32[64,1,8192]{2,0,1:T(8,128)} fusion(bf16[1,1848,8192]{2,1,0:T(8,128)(2,1)} %param.27, bf16[1,1848,8192]{2,1,0:T(8,128)(2,1)} %param.26, f32[64,1848]{1,0:T(8,128)S(1)} %fusion.28, bf16[64,1,8192]{2,0,1:T(8,128)(2,1)S(1)} %copy-done.2, f32[8192]{0:T(1024)S(1)} %bitcast.134, f32[64]{0:T(128)S(1)} %add_rsqrt_fusion.4), kind=kOutput, calls=%fused_computation.32 | convolution fusion | flops 3878343680 | bytes 64207104 | tf_op jit(solution)/shard_map/dot_general | solution.py:89
  95.5 35.7 %reduce-scatter.6.cloned.1.call-done = f32[64,1,1024]{2,0,1:T(8,128)} async-done(((f32[64,1,8192]{2,0,1:T(8,128)}), f32[64,1,1024]{2,0,1:T(8,128)}) %reduce-scatter.6.cloned.1.call-update) | async-done | bytes 262160 | tf_op jit(solution)/shard_map/reduce_scatter | solution.py:92
  131.1 1.0 add_convert_fusion.4
  132.1 3.4 collective-permute-start
  135.5 2.5 collective-permute-done
  138.0 0.7 slice_select_fusion.1
  138.7 0.3 reduce-scatter.8.cloned.1.call-start
  139.1 21.2 %all-gather.9.cloned.1.call-done = bf16[64,1,8192]{2,0,1:T(8,128)(2,1)} async-done(((bf16[64,1,1024]{2,0,1:T(8,128)(2,1)}), bf16[64,1,8192]{2,0,1:T(8,128)(2,1)}) %all-gather.9.cloned.1.call-update) | async-done | bytes 1048592 | tf_op jit(solution)/shard_map/all_gather | solution.py:84
  160.3 1.6 fusion.88
  161.9 14.8 %fusion.26 = f32[64,1848]{1,0:T(8,128)S(1)} fusion(bf16[1,1848,8192]{2,1,0:T(8,128)(2,1)} %param.25, bf16[64,1,8192]{2,0,1:T(8,128)(2,1)S(1)} %copy-done.6, f32[64]{0:T(128)S(1)} %add_rsqrt_fusion.3, f32[8192]{0:T(1024)S(1)} %bitcast.135), kind=kOutput, calls=%fused_computation.28 | convolution fusion | flops 1939865600 | bytes 31832320 | tf_op jit(solution)/shard_map/dot_general | solution.py:86
  176.7 25.7 %fusion.33 = f32[64,1,8192]{2,0,1:T(8,128)} fusion(bf16[1,1848,8192]{2,1,0:T(8,128)(2,1)} %param.27, bf16[1,1848,8192]{2,1,0:T(8,128)(2,1)} %param.26, f32[64,1848]{1,0:T(8,128)S(1)} %fusion.26, bf16[64,1,8192]{2,0,1:T(8,128)(2,1)S(1)} %copy-done.6, f32[64]{0:T(128)S(1)} %add_rsqrt_fusion.3, f32[8192]{0:T(1024)S(1)} %bitcast.136), kind=kOutput, calls=%fused_computation.33 | convolution fusion | flops 3878343680 | bytes 64207104 | tf_op jit(solution)/shard_map/dot_general | solution.py:89
  202.5 35.7 %reduce-scatter.8.cloned.1.call-done = f32[64,1,1024]{2,0,1:T(8,128)} async-done(((f32[64,1,8192]{2,0,1:T(8,128)}), f32[64,1,1024]{2,0,1:T(8,128)}) %reduce-scatter.8.cloned.1.call-update) | async-done | bytes 262160 | tf_op jit(solution)/shard_map/reduce_scatter | solution.py:92
  238.2 1.0 add_convert_fusion.3
  239.1 3.5 collective-permute-start.1
  242.6 2.5 collective-permute-done.1
  245.1 0.7 broadcast_select_fusion.2
  245.8 0.6 reduce-scatter.10.cloned.1.call-start
  246.4 20.8 %all-gather.11.cloned.1.call-done = bf16[64,1,8192]{2,0,1:T(8,128)(2,1)} async-done(((bf16[64,1,1024]{2,0,1:T(8,128)(2,1)}), bf16[64,1,8192]{2,0,1:T(8,128)(2,1)}) %all-gather.11.cloned.1.call-update) | async-done | bytes 1048592 | tf_op jit(solution)/shard_map/all_gather | solution.py:84
  267.1 1.6 fusion.91
  268.8 14.8 %fusion.24 = f32[64,1848]{1,0:T(8,128)S(1)} fusion(bf16[1,1848,8192]{2,1,0:T(8,128)(2,1)} %param.25, bf16[64,1,8192]{2,0,1:T(8,128)(2,1)S(1)} %copy-done.3, f32[64]{0:T(128)S(1)} %add_rsqrt_fusion.2, f32[8192]{0:T(1024)S(1)} %bitcast.137), kind=kOutput, calls=%fused_computation.26 | convolution fusion | flops 1939865600 | bytes 31832320 | tf_op jit(solution)/shard_map/dot_general | solution.py:86
  283.5 25.7 %fusion.36 = f32[64,1,8192]{2,0,1:T(8,128)} fusion(bf16[1,1848,8192]{2,1,0:T(8,128)(2,1)} %param.27, bf16[1,1848,8192]{2,1,0:T(8,128)(2,1)} %param.26, f32[64,1848]{1,0:T(8,128)S(1)} %fusion.24, bf16[64,1,8192]{2,0,1:T(8,128)(2,1)S(1)} %copy-done.3, f32[64]{0:T(128)S(1)} %add_rsqrt_fusion.2, f32[8192]{0:T(1024)S(1)} %bitcast.138), kind=kOutput, calls=%fused_computation.34 | convolution fusion | flops 3878343680 | bytes 64207104 | tf_op jit(solution)/shard_map/dot_general | solution.py:89
  309.3 35.8 %reduce-scatter.10.cloned.1.call-done = f32[64,1,1024]{2,0,1:T(8,128)} async-done(((f32[64,1,8192]{2,0,1:T(8,128)}), f32[64,1,1024]{2,0,1:T(8,128)}) %reduce-scatter.10.cloned.1.call-update) | async-done | bytes 262160 | tf_op jit(solution)/shard_map/reduce_scatter | solution.py:92
  345.1 1.0 add_convert_fusion.2
  346.1 3.4 collective-permute-start.2
  349.5 2.5 collective-permute-done.2
  352.0 0.7 broadcast_select_fusion.1
  352.7 0.2 reduce-scatter.12.cloned.1.call-start
  352.9 21.2 %all-gather.13.cloned.1.call-done = bf16[64,1,8192]{2,0,1:T(8,128)(2,1)} async-done(((bf16[64,1,1024]{2,0,1:T(8,128)(2,1)}), bf16[64,1,8192]{2,0,1:T(8,128)(2,1)}) %all-gather.13.cloned.1.call-update) | async-done | bytes 1048592 | tf_op jit(solution)/shard_map/all_gather | solution.py:84
  374.1 1.6 fusion.94
  375.7 14.8 %fusion.22 = f32[64,1848]{1,0:T(8,128)S(1)} fusion(bf16[1,1848,8192]{2,1,0:T(8,128)(2,1)} %param.25, bf16[64,1,8192]{2,0,1:T(8,128)(2,1)S(1)} %copy-done.4, f32[64]{0:T(128)S(1)} %add_rsqrt_fusion.1, f32[8192]{0:T(1024)S(1)} %bitcast.139), kind=kOutput, calls=%fused_computation.24 | convolution fusion | flops 1939865600 | bytes 31832320 | tf_op jit(solution)/shard_map/dot_general | solution.py:86
  390.5 25.7 %fusion.39 = f32[64,1,8192]{2,0,1:T(8,128)} fusion(bf16[1,1848,8192]{2,1,0:T(8,128)(2,1)} %param.27, bf16[1,1848,8192]{2,1,0:T(8,128)(2,1)} %param.26, f32[64,1848]{1,0:T(8,128)S(1)} %fusion.22, bf16[64,1,8192]{2,0,1:T(8,128)(2,1)S(1)} %copy-done.4, f32[64]{0:T(128)S(1)} %add_rsqrt_fusion.1, f32[8192]{0:T(1024)S(1)} %bitcast.140), kind=kOutput, calls=%fused_computation.35 | convolution fusion | flops 3878343680 | bytes 64207104 | tf_op jit(solution)/shard_map/dot_general | solution.py:89
  416.3 35.8 %reduce-scatter.12.cloned.1.call-done = f32[64,1,1024]{2,0,1:T(8,128)} async-done(((f32[64,1,8192]{2,0,1:T(8,128)}), f32[64,1,1024]{2,0,1:T(8,128)}) %reduce-scatter.12.cloned.1.call-update) | async-done | bytes 262160 | tf_op jit(solution)/shard_map/reduce_scatter | solution.py:92
  452.1 1.0 add_convert_fusion.1
  453.1 3.3 collective-permute-start.3
  456.3 2.5 collective-permute-done.3
  458.8 0.7 broadcast_select_fusion
  459.5 0.3 reduce-scatter.14.cloned.1.call-start
  459.8 21.2 %all-gather.15.cloned.1.call-done = bf16[64,1,8192]{2,0,1:T(8,128)(2,1)} async-done(((bf16[64,1,1024]{2,0,1:T(8,128)(2,1)}), bf16[64,1,8192]{2,0,1:T(8,128)(2,1)}) %all-gather.15.cloned.1.call-update) | async-done | bytes 1048592 | tf_op jit(solution)/shard_map/all_gather | solution.py:84
  481.0 1.6 fusion.97
  482.6 14.8 %fusion.20 = f32[64,1848]{1,0:T(8,128)S(1)} fusion(bf16[1,1848,8192]{2,1,0:T(8,128)(2,1)} %param.25, bf16[64,1,8192]{2,0,1:T(8,128)(2,1)S(1)} %copy-done.5, f32[64]{0:T(128)S(1)} %add_rsqrt_fusion, f32[8192]{0:T(1024)S(1)} %bitcast.141), kind=kOutput, calls=%fused_computation.22 | convolution fusion | flops 1939865600 | bytes 31832320 | tf_op jit(solution)/shard_map/dot_general | solution.py:86
  497.4 26.2 %fusion.42 = f32[64,1,8192]{2,0,1:T(8,128)} fusion(bf16[1,1848,8192]{2,1,0:T(8,128)(2,1)} %param.27, bf16[1,1848,8192]{2,1,0:T(8,128)(2,1)} %param.26, f32[64,1848]{1,0:T(8,128)S(1)} %fusion.20, bf16[64,1,8192]{2,0,1:T(8,128)(2,1)} %all-gather.15.cloned.1.call-done, f32[64]{0:T(128)S(1)} %add_rsqrt_fusion, f32[8192]{0:T(1024)S(1)} %bitcast.142), kind=kOutput, calls=%fused_computation.36 | convolution fusion | flops 3878343680 | bytes 64207104 | tf_op jit(solution)/shard_map/dot_general | solution.py:89
  523.7 35.8 %reduce-scatter.14.cloned.1.call-done = f32[64,1,1024]{2,0,1:T(8,128)} async-done(((f32[64,1,8192]{2,0,1:T(8,128)}), f32[64,1,1024]{2,0,1:T(8,128)}) %reduce-scatter.14.cloned.1.call-update) | async-done | bytes 262160 | tf_op jit(solution)/shard_map/reduce_scatter | solution.py:92
  559.5 1.0 add_convert_fusion
  560.5 0.7 maximum_select_fusion
  561.2 42.9 %all-reduce.2.cloned.1.call-done = bf16[64,2,1024]{2,0,1:T(8,128)(2,1)} async-done(((bf16[64,2,1024]{2,0,1:T(8,128)(2,1)}), bf16[64,2,1024]{2,0,1:T(8,128)(2,1)}) %all-reduce.2.cloned.1.call-update) | async-done | bytes 262160 | tf_op jit(solution)/shard_map/psum | solution.py:15
  604.1 0.8 constant_dynamic-slice_fusion
  604.9 0.7 copy.27
  (53 shorter events, 0.8 us)
Async XLA Ops:
  6.5 19.4 %copy-start = (bf16[1280,1024]{1,0:T(8,128)(2,1)S(1)}, bf16[1280,1024]{1,0:T(8,128)(2,1)}, u32[]{:S(2)}) copy-start(bf16[1280,1024]{1,0:T(8,128)(2,1)} %param.21) | copy-start | bytes 7864324
  6.5 22.4 %copy-start.9 = (bf16[64,2,1024]{2,1,0:T(2,128)(2,1)S(1)}, bf16[64,2,1024]{2,1,0:T(2,128)(2,1)}, u32[]{:S(2)}) copy-start(bf16[64,2,1024]{2,1,0:T(2,128)(2,1)} %param.23) | copy-start | bytes 786436
  6.5 46.7 %all-gather.7.cloned.1.call-start = ((), (), s32[]{:S(2)}) async-start(), calls=%async_computation.5 | async-start | bytes 1179648 | tf_op jit(solution)/shard_map/all_gather | solution.py:84
  27.1 27.7 %copy-start.7 = (f32[1,8192]{1,0:T(1,128)S(1)}, f32[1,8192]{1,0:T(1,128)}, u32[]{:S(2)}) copy-start(f32[1,8192]{1,0:T(1,128)} %param.24) | copy-start | bytes 98308
  29.8 101.3 %reduce-scatter.6.cloned.1.call-start = ((), (), s32[]{:S(2)}) async-start(), calls=%async_computation.6 | async-start | bytes 2359296 | tf_op jit(solution)/shard_map/reduce_scatter | solution.py:92
  53.2 1.6 copy-start.2
  95.4 64.8 %all-gather.9.cloned.1.call-start = ((), (), s32[]{:S(2)}) async-start(), calls=%async_computation.7 | async-start | bytes 1179648 | tf_op jit(solution)/shard_map/all_gather | solution.py:84
  132.1 5.9 collective-permute-start
  138.7 99.4 %reduce-scatter.8.cloned.1.call-start = ((), (), s32[]{:S(2)}) async-start(), calls=%async_computation.8 | async-start | bytes 2359296 | tf_op jit(solution)/shard_map/reduce_scatter | solution.py:92
  160.3 1.6 copy-start.6
  202.4 35.8 %copy-start.8 = (bf16[64,1,1024]{2,0,1:T(8,128)(2,1)S(1)}, bf16[64,1,1024]{2,0,1:T(8,128)(2,1)}, u32[]{:S(2)}) copy-start(bf16[64,1,1024]{2,0,1:T(8,128)(2,1)} %slice_select_fusion.1) | copy-start | bytes 393220
  202.4 64.7 %all-gather.11.cloned.1.call-start = ((), (), s32[]{:S(2)}) async-start(), calls=%async_computation.9 | async-start | bytes 1179648 | tf_op jit(solution)/shard_map/all_gather | solution.py:84
  239.1 6.0 collective-permute-start.1
  245.8 99.4 %reduce-scatter.10.cloned.1.call-start = ((), (), s32[]{:S(2)}) async-start(), calls=%async_computation.10 | async-start | bytes 2359296 | tf_op jit(solution)/shard_map/reduce_scatter | solution.py:92
  267.1 1.6 copy-start.3
  309.3 64.8 %all-gather.13.cloned.1.call-start = ((), (), s32[]{:S(2)}) async-start(), calls=%async_computation.11 | async-start | bytes 1179648 | tf_op jit(solution)/shard_map/all_gather | solution.py:84
  346.1 5.9 collective-permute-start.2
  352.7 99.4 %reduce-scatter.12.cloned.1.call-start = ((), (), s32[]{:S(2)}) async-start(), calls=%async_computation.12 | async-start | bytes 2359296 | tf_op jit(solution)/shard_map/reduce_scatter | solution.py:92
  374.1 1.6 copy-start.4
  416.2 64.8 %all-gather.15.cloned.1.call-start = ((), (), s32[]{:S(2)}) async-start(), calls=%async_computation.13 | async-start | bytes 1179648 | tf_op jit(solution)/shard_map/all_gather | solution.py:84
  453.1 5.8 collective-permute-start.3
  459.5 100.0 %reduce-scatter.14.cloned.1.call-start = ((), (), s32[]{:S(2)}) async-start(), calls=%async_computation.14 | async-start | bytes 2359296 | tf_op jit(solution)/shard_map/reduce_scatter | solution.py:92
  481.0 1.6 copy-start.5
  497.4 108.2 %copy-start.1 = (bf16[1280,1024]{1,0:T(8,128)(2,1)S(1)}, bf16[1280,1024]{1,0:T(8,128)(2,1)}, u32[]{:S(2)}) copy-start(bf16[1280,1024]{1,0:T(8,128)(2,1)} %param.21) | copy-start | bytes 7864324
  523.6 80.5 %all-reduce.2.cloned.1.call-start = ((), (), s32[]{:S(2)}) async-start(), calls=%async_computation.15 | async-start | bytes 524288 | tf_op jit(solution)/shard_map/psum | solution.py:15
Sparse Core Ops, SparseCore 0:
  29.9 23.2 all-gather.6
  95.5 35.5 reduce-scatter.5
  138.8 21.3 all-gather.8
  202.5 35.5 reduce-scatter.7
  245.9 21.1 all-gather.10
  309.4 35.6 reduce-scatter.9
  352.8 21.2 all-gather.12
  416.3 35.6 reduce-scatter.11
  459.6 21.2 all-gather.14
  523.7 35.6 reduce-scatter.13
  562.4 41.6 all-reduce.1
where the time goes:
time: 620 us; the launch traced here: 612 us
  waiting for transfers between devices  340 us (55%)
  matrix products  204 us (33%)
  other arithmetic  19.8 us (3%)
  blocking collectives  15.8 us (3%)
  starting transfers between devices  15.1 us (2%)
  between operations  13.8 us (2%)
    reduce_scatter x5, waiting for transfers between devices, on_device(): lax.psum_scatter(partial_sum, 'fsdp', scatter_dimension=2, tiled=True)  179 us
    dot_general x5, matrix products, on_device(): jnp.dot(hidden, down_w, preferred_element_type=jnp.float32)  129 us
    all_gather x5, waiting for transfers between devices, on_device(): whole = lax.all_gather(current, 'fsdp', axis=2, tiled=True)  108 us
    dot_general x5, matrix products, on_device(): lax.dot_general(layer_normed, gate_w, dims, preferred_element_type=jnp.fl...  73.8 us
    psum x1, waiting for transfers between devices, from_root(): return lax.psum(kept, axis)  42.9 us
    all_gather x1, blocking collectives, on_device(): lax.all_gather(audio_ln, 'fsdp', axis=0, tiled=True)  15.8 us
    ppermute x4, starting transfers between devices, from_behind(): lax.ppermute(value, axis, [(source, source + steps) for source in range(i...  13.5 us
  transfers between devices with their start and end apart: 15, of which 15 were waited for; matrix products, arithmetic and copies ran while one was open for 0% of the time, Pallas kernels for 0%

commit v1 on v0

--- a/solution.py
+++ b/solution.py
@@ -81,7 +81,8 @@
         else:
             fresh = zero_rows
         current = jnp.where(first_section, fresh, incoming)
-        whole = lax.all_gather(current, "fsdp", axis=2, tiled=True)
+        pieces = lax.all_gather(current, "fsdp")
+        whole = jnp.concatenate(pieces, axis=2)
         layer_normed = rms_scaled(whole, gain).reshape(-1, width)
         gate = lax.dot_general(layer_normed, gate_w, dims, preferred_element_type=jnp.float32)
         up = lax.dot_general(layer_normed, up_w, dims, preferred_element_type=jnp.float32)

time: 620 us -> 647 us (1.044)
  local copies, waits for them, and re-layouts: 4.38 us -> 27.1 us
  other arithmetic: 19.8 us -> 26.9 us
    convert_element_type x0 -> x10, local copies, waits for them, and re-layouts: none -> 21.6 us  [rms_scaled(): values = stream.astype(jnp.float32)]
    convert_element_type x0 -> x5, other arithmetic: none -> 7.34 us  [rms_scaled(): values = stream.astype(jnp.float32)]
where the time goes in v1:
time: 647 us; the launch traced here: 640 us
  waiting for transfers between devices  340 us (53%)
  matrix products  201 us (31%)
  local copies, waits for them, and re-layouts  27.1 us (4%)
  other arithmetic  26.9 us (4%)
  blocking collectives  15.8 us (2%)
  starting transfers between devices  14.9 us (2%)
  between operations  13.8 us (2%)
    reduce_scatter x5, waiting for transfers between devices, on_device(): lax.psum_scatter(partial_sum, 'fsdp', scatter_dimension=2, tiled=True)  179 us
    dot_general x5, matrix products, on_device(): jnp.dot(hidden, down_w, preferred_element_type=jnp.float32)  129 us
    all_gather x5, waiting for transfers between devices, on_device(): pieces = lax.all_gather(current, 'fsdp')  108 us
    dot_general x5, matrix products, on_device(): lax.dot_general(layer_normed, gate_w, dims, preferred_element_type=jnp.fl...  71 us
    psum x1, waiting for transfers between devices, from_root(): return lax.psum(kept, axis)  42.9 us
    convert_element_type x10, local copies, waits for them, and re-layouts, rms_scaled(): values = stream.astype(jnp.float32)  21.6 us
    all_gather x1, blocking collectives, on_device(): lax.all_gather(audio_ln, 'fsdp', axis=0, tiled=True)  15.8 us
    ppermute x4, starting transfers between devices, from_behind(): lax.ppermute(value, axis, [(source, source + steps) for source in range(i...  13.3 us
  transfers between devices with their start and end apart: 15, of which 15 were waited for; matrix products, arithmetic and copies ran while one was open for 0% of the time, Pallas kernels for 0%

profile of v1, /device:TPU:0, one launch (start us, length us, event | category | flops | bytes accessed | tf_op | source)
XLA Modules:
  0.0 639.7 jit_solution(10589703348239563159)
XLA Ops:
  6.6 0.9 broadcast_compare_fusion
  7.5 0.7 iota_add_fusion
  9.2 0.7 reshape.900
  10.3 0.8 fusion.130
  11.1 15.8 %all-gather.5 = bf16[8,2,1280]{2,1,0:T(2,128)(2,1)S(1)} all-gather(bf16[1,2,1280]{2,1,0:T(2,128)(2,1)S(1)} %fusion.130), channel_id=1, replica_groups=mesh['section'=4,'fsdp'=8] {'fsdp'}, dimensions={0}, use_global_device_ids=true | all-gather | bytes 46080 | tf_op jit(solution)/shard_map/all_gather | solution.py:52
  26.9 1.1 fusion.85
  28.1 0.8 scatter_custom_fusion.1
  29.9 23.4 %all-gather.12.cloned.1.call-done = bf16[512,1,1024]{2,0,1:T(8,128)(2,1)} async-done(((bf16[64,1,1024]{2,0,1:T(8,128)(2,1)}), bf16[512,1,1024]{2,0,1:T(8,128)(2,1)}) %all-gather.12.cloned.1.call-update) | async-done | bytes 1048592 | tf_op jit(solution)/shard_map/all_gather | solution.py:84
  53.3 1.5 multiply_reduce_fusion.4
  54.8 1.5 bitcast_convert_fusion.4
  56.3 2.6 copy.60
  58.8 1.8 reshape.901
  60.6 14.2 %fusion.28 = f32[64,1848]{1,0:T(8,128)S(1)} fusion(bf16[1,1848,8192]{2,1,0:T(8,128)(2,1)} %param.25, f32[64,1,1,1,1,1,8192]{6,0,5,4,3,2,1:T(8,128)S(1)} %reshape.901, f32[8192]{0:T(1024)S(1)} %bitcast.185, f32[64]{0:T(128)S(1)} %add_rsqrt_fusion.4), kind=kOutput, calls=%fused_computation.30 | convolution fusion | flops 1939341312 | bytes 32880896 | tf_op jit(solution)/shard_map/dot_general | solution.py:87
  74.8 25.7 %fusion.30 = f32[64,1,8192]{2,0,1:T(8,128)} fusion(bf16[1,1848,8192]{2,1,0:T(8,128)(2,1)} %param.27, bf16[1,1848,8192]{2,1,0:T(8,128)(2,1)} %param.26, f32[64,1848]{1,0:T(8,128)S(1)} %fusion.28, f32[64,1,1,1,1,1,8192]{6,0,5,4,3,2,1:T(8,128)S(1)} %reshape.901, f32[8192]{0:T(1024)S(1)} %bitcast.186, f32[64]{0:T(128)S(1)} %add_rsqrt_fusion.4), kind=kOutput, calls=%fused_computation.32 | convolution fusion | flops 3877819392 | bytes 65255680 | tf_op jit(solution)/shard_map/dot_general | solution.py:90
  100.6 35.8 %reduce-scatter.6.cloned.1.call-done = f32[64,1,1024]{2,0,1:T(8,128)} async-done(((f32[64,1,8192]{2,0,1:T(8,128)}), f32[64,1,1024]{2,0,1:T(8,128)}) %reduce-scatter.6.cloned.1.call-update) | async-done | bytes 262160 | tf_op jit(solution)/shard_map/reduce_scatter | solution.py:93
  136.4 1.0 add_convert_fusion.4
  137.3 3.3 collective-permute-start
  140.7 2.5 collective-permute-done
  144.2 21.1 %all-gather.14.cloned.1.call-done = bf16[512,1,1024]{2,0,1:T(8,128)(2,1)} async-done(((bf16[64,1,1024]{2,0,1:T(8,128)(2,1)}), bf16[512,1,1024]{2,0,1:T(8,128)(2,1)}) %all-gather.14.cloned.1.call-update) | async-done | bytes 1048592 | tf_op jit(solution)/shard_map/all_gather | solution.py:84
  165.3 1.5 multiply_reduce_fusion.3
  166.9 1.5 bitcast_convert_fusion.3
  168.3 2.6 copy.59
  170.9 1.7 reshape.902
  172.7 14.2 %fusion.26 = f32[64,1848]{1,0:T(8,128)S(1)} fusion(bf16[1,1848,8192]{2,1,0:T(8,128)(2,1)} %param.25, f32[64,1,1,1,1,1,8192]{6,0,5,4,3,2,1:T(8,128)S(1)} %reshape.902, f32[64]{0:T(128)S(1)} %add_rsqrt_fusion.3, f32[8192]{0:T(1024)S(1)} %bitcast.187), kind=kOutput, calls=%fused_computation.28 | convolution fusion | flops 1939341312 | bytes 32880896 | tf_op jit(solution)/shard_map/dot_general | solution.py:87
  186.9 25.7 %fusion.33 = f32[64,1,8192]{2,0,1:T(8,128)} fusion(bf16[1,1848,8192]{2,1,0:T(8,128)(2,1)} %param.27, bf16[1,1848,8192]{2,1,0:T(8,128)(2,1)} %param.26, f32[64,1848]{1,0:T(8,128)S(1)} %fusion.26, f32[64,1,1,1,1,1,8192]{6,0,5,4,3,2,1:T(8,128)S(1)} %reshape.902, f32[64]{0:T(128)S(1)} %add_rsqrt_fusion.3, f32[8192]{0:T(1024)S(1)} %bitcast.188), kind=kOutput, calls=%fused_computation.33 | convolution fusion | flops 3877819392 | bytes 65255680 | tf_op jit(solution)/shard_map/dot_general | solution.py:90
  212.6 35.7 %reduce-scatter.8.cloned.1.call-done = f32[64,1,1024]{2,0,1:T(8,128)} async-done(((f32[64,1,8192]{2,0,1:T(8,128)}), f32[64,1,1024]{2,0,1:T(8,128)}) %reduce-scatter.8.cloned.1.call-update) | async-done | bytes 262160 | tf_op jit(solution)/shard_map/reduce_scatter | solution.py:93
  248.4 1.0 add_convert_fusion.3
  249.4 3.4 collective-permute-start.1
  252.7 2.5 collective-permute-done.1
  256.5 20.9 %all-gather.16.cloned.1.call-done = bf16[512,1,1024]{2,0,1:T(8,128)(2,1)} async-done(((bf16[64,1,1024]{2,0,1:T(8,128)(2,1)}), bf16[512,1,1024]{2,0,1:T(8,128)(2,1)}) %all-gather.16.cloned.1.call-update) | async-done | bytes 1048592 | tf_op jit(solution)/shard_map/all_gather | solution.py:84
  277.4 1.5 multiply_reduce_fusion.2
  279.0 1.5 bitcast_convert_fusion.2
  280.4 2.6 copy.58
  283.0 1.7 reshape.903
  284.7 14.2 %fusion.24 = f32[64,1848]{1,0:T(8,128)S(1)} fusion(bf16[1,1848,8192]{2,1,0:T(8,128)(2,1)} %param.25, f32[64,1,1,1,1,1,8192]{6,0,5,4,3,2,1:T(8,128)S(1)} %reshape.903, f32[64]{0:T(128)S(1)} %add_rsqrt_fusion.2, f32[8192]{0:T(1024)S(1)} %bitcast.189), kind=kOutput, calls=%fused_computation.26 | convolution fusion | flops 1939341312 | bytes 32880896 | tf_op jit(solution)/shard_map/dot_general | solution.py:87
  299.0 25.7 %fusion.36 = f32[64,1,8192]{2,0,1:T(8,128)} fusion(bf16[1,1848,8192]{2,1,0:T(8,128)(2,1)} %param.27, bf16[1,1848,8192]{2,1,0:T(8,128)(2,1)} %param.26, f32[64,1848]{1,0:T(8,128)S(1)} %fusion.24, f32[64,1,1,1,1,1,8192]{6,0,5,4,3,2,1:T(8,128)S(1)} %reshape.903, f32[64]{0:T(128)S(1)} %add_rsqrt_fusion.2, f32[8192]{0:T(1024)S(1)} %bitcast.190), kind=kOutput, calls=%fused_computation.34 | convolution fusion | flops 3877819392 | bytes 65255680 | tf_op jit(solution)/shard_map/dot_general | solution.py:90
  324.7 35.8 %reduce-scatter.10.cloned.1.call-done = f32[64,1,1024]{2,0,1:T(8,128)} async-done(((f32[64,1,8192]{2,0,1:T(8,128)}), f32[64,1,1024]{2,0,1:T(8,128)}) %reduce-scatter.10.cloned.1.call-update) | async-done | bytes 262160 | tf_op jit(solution)/shard_map/reduce_scatter | solution.py:93
  360.5 1.0 add_convert_fusion.2
  361.5 3.3 collective-permute-start.2
  364.8 2.5 collective-permute-done.2
  368.2 21.4 %all-gather.18.cloned.1.call-done = bf16[512,1,1024]{2,0,1:T(8,128)(2,1)} async-done(((bf16[64,1,1024]{2,0,1:T(8,128)(2,1)}), bf16[512,1,1024]{2,0,1:T(8,128)(2,1)}) %all-gather.18.cloned.1.call-update) | async-done | bytes 1048592 | tf_op jit(solution)/shard_map/all_gather | solution.py:84
  389.6 1.5 multiply_reduce_fusion.1
  391.1 1.5 bitcast_convert_fusion.1
  392.6 2.6 copy.57
  395.2 1.7 reshape.904
  396.9 14.2 %fusion.22 = f32[64,1848]{1,0:T(8,128)S(1)} fusion(bf16[1,1848,8192]{2,1,0:T(8,128)(2,1)} %param.25, f32[64,1,1,1,1,1,8192]{6,0,5,4,3,2,1:T(8,128)S(1)} %reshape.904, f32[64]{0:T(128)S(1)} %add_rsqrt_fusion.1, f32[8192]{0:T(1024)S(1)} %bitcast.191), kind=kOutput, calls=%fused_computation.24 | convolution fusion | flops 1939341312 | bytes 32880896 | tf_op jit(solution)/shard_map/dot_general | solution.py:87
  411.1 25.7 %fusion.39 = f32[64,1,8192]{2,0,1:T(8,128)} fusion(bf16[1,1848,8192]{2,1,0:T(8,128)(2,1)} %param.27, bf16[1,1848,8192]{2,1,0:T(8,128)(2,1)} %param.26, f32[64,1848]{1,0:T(8,128)S(1)} %fusion.22, f32[64,1,1,1,1,1,8192]{6,0,5,4,3,2,1:T(8,128)S(1)} %reshape.904, f32[64]{0:T(128)S(1)} %add_rsqrt_fusion.1, f32[8192]{0:T(1024)S(1)} %bitcast.192), kind=kOutput, calls=%fused_computation.35 | convolution fusion | flops 3877819392 | bytes 65255680 | tf_op jit(solution)/shard_map/dot_general | solution.py:90
  436.9 35.8 %reduce-scatter.12.cloned.1.call-done = f32[64,1,1024]{2,0,1:T(8,128)} async-done(((f32[64,1,8192]{2,0,1:T(8,128)}), f32[64,1,1024]{2,0,1:T(8,128)}) %reduce-scatter.12.cloned.1.call-update) | async-done | bytes 262160 | tf_op jit(solution)/shard_map/reduce_scatter | solution.py:93
  472.7 1.0 add_convert_fusion.1
  473.6 3.4 collective-permute-start.3
  477.0 2.5 collective-permute-done.3
  480.5 21.1 %all-gather.20.cloned.1.call-done = bf16[512,1,1024]{2,0,1:T(8,128)(2,1)} async-done(((bf16[64,1,1024]{2,0,1:T(8,128)(2,1)}), bf16[512,1,1024]{2,0,1:T(8,128)(2,1)}) %all-gather.20.cloned.1.call-update) | async-done | bytes 1048592 | tf_op jit(solution)/shard_map/all_gather | solution.py:84
  501.6 1.5 multiply_reduce_fusion
  503.2 1.5 bitcast_convert_fusion
  504.6 2.6 copy.56
  507.2 1.7 reshape.905
  509.0 1.3 copy-done.2
  510.2 14.2 %fusion.20 = f32[64,1848]{1,0:T(8,128)S(1)} fusion(bf16[1,1848,8192]{2,1,0:T(8,128)(2,1)} %param.25, f32[64,1,1,1,1,1,8192]{6,0,5,4,3,2,1:T(8,128)S(1)} %reshape.905, f32[64]{0:T(128)S(1)} %add_rsqrt_fusion, f32[8192]{0:T(1024)S(1)} %bitcast.193), kind=kOutput, calls=%fused_computation.22 | convolution fusion | flops 1939341312 | bytes 32880896 | tf_op jit(solution)/shard_map/dot_general | solution.py:87
  524.5 26.5 %fusion.42 = f32[64,1,8192]{2,0,1:T(8,128)} fusion(bf16[1,1848,8192]{2,1,0:T(8,128)(2,1)} %param.27, bf16[1,1848,8192]{2,1,0:T(8,128)(2,1)} %param.26, f32[64,1848]{1,0:T(8,128)S(1)} %fusion.20, f32[64,1,1,1,1,1,8192]{6,0,5,4,3,2,1:T(8,128)} %copy-done.2, f32[64]{0:T(128)S(1)} %add_rsqrt_fusion, f32[8192]{0:T(1024)S(1)} %bitcast.194), kind=kOutput, calls=%fused_computation.36 | convolution fusion | flops 3877819392 | bytes 65255680 | tf_op jit(solution)/shard_map/dot_general | solution.py:90
  551.1 35.7 %reduce-scatter.14.cloned.1.call-done = f32[64,1,1024]{2,0,1:T(8,128)} async-done(((f32[64,1,8192]{2,0,1:T(8,128)}), f32[64,1,1024]{2,0,1:T(8,128)}) %reduce-scatter.14.cloned.1.call-update) | async-done | bytes 262160 | tf_op jit(solution)/shard_map/reduce_scatter | solution.py:93
  586.7 1.0 add_convert_fusion
  587.7 0.7 maximum_select_fusion
  588.5 42.9 %all-reduce.2.cloned.1.call-done = bf16[64,2,1024]{2,0,1:T(8,128)(2,1)} async-done(((bf16[64,2,1024]{2,0,1:T(8,128)(2,1)}), bf16[64,2,1024]{2,0,1:T(8,128)(2,1)}) %all-reduce.2.cloned.1.call-update) | async-done | bytes 262160 | tf_op jit(solution)/shard_map/psum | solution.py:15
  631.4 0.8 constant_dynamic-slice_fusion
  (60 shorter events, 7.5 us)
Async XLA Ops:
  6.5 20.4 %copy-start = (bf16[1280,1024]{1,0:T(8,128)(2,1)S(1)}, bf16[1280,1024]{1,0:T(8,128)(2,1)}, u32[]{:S(2)}) copy-start(bf16[1280,1024]{1,0:T(8,128)(2,1)} %param.21) | copy-start | bytes 7864324
  6.5 22.4 %copy-start.5 = (bf16[64,2,1024]{2,1,0:T(2,128)(2,1)S(1)}, bf16[64,2,1024]{2,1,0:T(2,128)(2,1)}, u32[]{:S(2)}) copy-start(bf16[64,2,1024]{2,1,0:T(2,128)(2,1)} %param.23) | copy-start | bytes 786436
  6.5 46.7 %all-gather.12.cloned.1.call-start = ((), (), s32[]{:S(2)}) async-start(), calls=%async_computation.11 | async-start | bytes 1179648 | tf_op jit(solution)/shard_map/all_gather | solution.py:84
  29.8 106.5 %reduce-scatter.6.cloned.1.call-start = ((), (), s32[]{:S(2)}) async-start(), calls=%async_computation.5 | async-start | bytes 2359296 | tf_op jit(solution)/shard_map/reduce_scatter | solution.py:93
  58.8 1.8 copy-start.3
  100.5 64.8 %all-gather.14.cloned.1.call-start = ((), (), s32[]{:S(2)}) async-start(), calls=%async_computation.12 | async-start | bytes 1179648 | tf_op jit(solution)/shard_map/all_gather | solution.py:84
  137.3 5.8 collective-permute-start
  143.8 104.5 %reduce-scatter.8.cloned.1.call-start = ((), (), s32[]{:S(2)}) async-start(), calls=%async_computation.6 | async-start | bytes 2359296 | tf_op jit(solution)/shard_map/reduce_scatter | solution.py:93
  212.6 35.8 %copy-start.4 = (bf16[64,1,1024]{2,0,1:T(8,128)(2,1)S(1)}, bf16[64,1,1024]{2,0,1:T(8,128)(2,1)}, u32[]{:S(2)}) copy-start(bf16[64,1,1024]{2,0,1:T(8,128)(2,1)} %slice_select_fusion.1) | copy-start | bytes 393220
  212.6 64.8 %all-gather.16.cloned.1.call-start = ((), (), s32[]{:S(2)}) async-start(), calls=%async_computation.13 | async-start | bytes 1179648 | tf_op jit(solution)/shard_map/all_gather | solution.py:84
  249.4 5.9 collective-permute-start.1
  255.9 104.6 %reduce-scatter.10.cloned.1.call-start = ((), (), s32[]{:S(2)}) async-start(), calls=%async_computation.7 | async-start | bytes 2359296 | tf_op jit(solution)/shard_map/reduce_scatter | solution.py:93
  324.7 64.9 %all-gather.18.cloned.1.call-start = ((), (), s32[]{:S(2)}) async-start(), calls=%async_computation.14 | async-start | bytes 1179648 | tf_op jit(solution)/shard_map/all_gather | solution.py:84
  361.5 5.8 collective-permute-start.2
  368.0 104.7 %reduce-scatter.12.cloned.1.call-start = ((), (), s32[]{:S(2)}) async-start(), calls=%async_computation.8 | async-start | bytes 2359296 | tf_op jit(solution)/shard_map/reduce_scatter | solution.py:93
  436.8 64.8 %all-gather.20.cloned.1.call-start = ((), (), s32[]{:S(2)}) async-start(), calls=%async_computation.15 | async-start | bytes 1179648 | tf_op jit(solution)/shard_map/all_gather | solution.py:84
  473.6 5.9 collective-permute-start.3
  480.2 106.5 %reduce-scatter.14.cloned.1.call-start = ((), (), s32[]{:S(2)}) async-start(), calls=%async_computation.9 | async-start | bytes 2359296 | tf_op jit(solution)/shard_map/reduce_scatter | solution.py:93
  508.9 1.3 copy-start.2
  524.4 108.5 %copy-start.1 = (bf16[1280,1024]{1,0:T(8,128)(2,1)S(1)}, bf16[1280,1024]{1,0:T(8,128)(2,1)}, u32[]{:S(2)}) copy-start(bf16[1280,1024]{1,0:T(8,128)(2,1)} %param.21) | copy-start | bytes 7864324
  551.0 80.4 %all-reduce.2.cloned.1.call-start = ((), (), s32[]{:S(2)}) async-start(), calls=%async_computation.10 | async-start | bytes 524288 | tf_op jit(solution)/shard_map/psum | solution.py:15
Sparse Core Ops, SparseCore 0:
  29.9 23.2 all-gather.11
  100.7 35.6 reduce-scatter.5
  144.0 21.3 all-gather.13
  212.7 35.6 reduce-scatter.7
  256.0 21.3 all-gather.15
  324.8 35.6 reduce-scatter.9
  368.1 21.4 all-gather.17
  437.0 35.6 reduce-scatter.11
  480.3 21.2 all-gather.19
  551.1 35.5 reduce-scatter.13
  589.7 41.6 all-reduce.1
